TPU v7x, 32 devices: a whole 2x2x4 slice. The times are simulated.
32 devices in a mesh: groups: 2 (over y), sec: 4 (over z), strip: 4 (over x, core).
Axes of the slice: x: 2, y: 2, z: 4, core: 2. Of those that a mesh axis runs over, the one named last changes fastest.
Arguments:
- sections: bfloat16 [4, 256, 1024], P('sec', 'strip', 'groups'), parts along dimension 2, may hold values from -40 to 40
- mask_fine: int32 [4, 8, 32], P('sec', 'strip', 'groups'), parts along dimension 2, may hold values 0 or 1
- mask_coarse: int32 [4, 4, 16], P('sec', 'strip', 'groups'), parts along dimension 2, may hold values 0 or 1
Outputs:
- corr_fine: float32 [4, 2, 8, 32, 1024], P('sec', None, 'strip', 'groups'), parts along dimension 3
- corr_coarse: float32 [4, 2, 4, 16, 1024], P('sec', None, 'strip', 'groups'), parts along dimension 3
There are 2 independent parts, one for each index of `groups`. A program takes and returns all parts, laid end to end along the dimension named above; each array names one. Nothing has to cross between parts.
All inputs are finite; a program needn't handle non-finite values. No bound on the sum of `mask_fine` or of `mask_coarse` on one device may be relied on, other than what follows from the above.
Results may differ from a plain program's by a relative error of at most 0.0039.
Values may be sent and summed in bfloat16 or wider, within the bound.
A program may use at most 64 MiB of HBM per device.

v0:
```python
import functools

import jax
import jax.numpy as jnp
import numpy as np
from jax import lax
from jax.experimental import pallas as pl
from jax.experimental.pallas import tpu as pltpu
from jax.sharding import PartitionSpec as P

PATCH = 64
STRIDE = 32
WINDOW = 32
HALF = PATCH // 2 + 1
KP = 40
CHUNKS = 4
LANES = 128
F32 = jnp.float32
BF16 = jnp.bfloat16
MESH = pl.DeviceIdType.MESH


def trig(phase):
    angle = 2.0 * np.pi / PATCH * np.mod(phase, PATCH)
    return np.round(np.cos(angle), 12), np.round(np.sin(angle), 12)


def split(table):
    high = np.asarray(table, np.float32).astype(BF16)
    low = (np.asarray(table, np.float64) - high.astype(np.float64)).astype(np.float32).astype(BF16)
    return high, low


def block_diagonal(block, count):
    return np.kron(np.eye(count), block)


def tables(strip_rows):
    fine_rows = strip_rows // STRIDE
    coarse_rows = strip_rows // (2 * STRIDE)
    height = strip_rows + PATCH
    k = np.arange(KP)[:, None]
    keep = (k < HALF).astype(np.float64)
    x = np.arange(height)[None, :]
    units = []
    for i in range(fine_rows):
        c, s = trig(k * (x - STRIDE * i))
        inside = ((x >= STRIDE * i) & (x < STRIDE * i + PATCH)) * keep
        units += [c * inside, -s * inside]
    for i in range(coarse_rows):
        xc = x // 2 - STRIDE * i
        c, s = trig(k * xc)
        inside = ((xc >= 0) & (xc < PATCH)) * keep * 0.25
        units += [c * inside, -s * inside]
    a_high, a_low = split(np.concatenate(units, axis=0))
    first = np.concatenate([a_high, a_low], axis=1)

    freq = np.arange(PATCH)[None, :]
    y = np.arange(STRIDE)[:, None]
    c, s = trig(y * freq)

    def second(c, s, count):
        c, s = block_diagonal(c, count), block_diagonal(s, count)
        return split(np.block([[c, -s], [s, c]]))

    fine_w = second(c, s, LANES // STRIDE)
    coarse_w = second(np.repeat(c, 2, axis=0), np.repeat(s, 2, axis=0), LANES // (2 * STRIDE))

    shift = np.arange(WINDOW) - WINDOW // 2
    c, s = trig(np.arange(PATCH)[:, None] * shift[None, :])
    c, s = block_diagonal(c, 4), block_diagonal(s, 4)
    inverse = split(np.block([[c, s], [-s, c]]))

    weight = np.where((k == 0) | (k == PATCH // 2), 1.0, 2.0) * keep
    c, s = trig(shift[:, None] * np.arange(KP)[None, :])
    last_high, last_low = split(np.concatenate([c * weight.T, -s * weight.T], axis=1))
    last = np.concatenate([last_high, last_high, last_low], axis=1)
    energy = np.kron(np.eye(4), np.ones((PATCH, WINDOW)))
    return [
        first,
        *fine_w,
        *coarse_w,
        *inverse,
        last,
        np.asarray(energy, np.float32),
        np.asarray(np.broadcast_to(weight, (KP, LANES)), np.float32),
    ]


def split_value(value):
    high = value.astype(BF16)
    return high, (value - high.astype(F32)).astype(BF16)


def matmul(a, b):
    return jnp.dot(a, b, preferred_element_type=F32)


def section_spectra(pixels, first, fine_w, coarse_w, fine_rows, coarse_rows):
    half = matmul(first, jnp.concatenate([pixels, pixels], axis=0))
    width = half.shape[1]
    tiles = width // LANES
    row = lax.broadcasted_iota(jnp.int32, (KP, width), 0)
    fine_in, coarse_in = [], []
    for unit in range(fine_rows + coarse_rows):
        real = half[2 * KP * unit : 2 * KP * unit + KP]
        imag = half[2 * KP * unit + KP : 2 * KP * (unit + 1)]
        sums = real[0:1]
        high = sums.astype(BF16).astype(F32)
        middle = (sums - high).astype(BF16).astype(F32)
        low = sums - high - middle
        real = jnp.where(row == 0, high, real)
        real = jnp.where(row == HALF, middle, real)
        real = jnp.where(row == HALF + 1, low, real)
        target = fine_in if unit < fine_rows else coarse_in
        for tile in range(tiles):
            at = slice(LANES * tile, LANES * (tile + 1))
            target.append(jnp.concatenate([real[:, at], imag[:, at]], axis=1))

    def transform(parts, weights):
        high, low = split_value(jnp.concatenate(parts, axis=0))
        w_high, w_low = weights
        return matmul(high, w_high) + matmul(low, w_high) + matmul(high, w_low)

    fine = transform(fine_in, fine_w)
    coarse = transform(coarse_in, coarse_w)
    wide = 2 * LANES
    lane = lax.broadcasted_iota(jnp.int32, (KP, wide), 1)
    krow = lax.broadcasted_iota(jnp.int32, (KP, wide), 0)
    sign = jnp.where(lane % 2 == 0, 1.0, -1.0).astype(F32)
    dc = (krow == 0) & (lane % PATCH == 0)

    def finish(parts, rows):
        count = len(parts) // rows
        rolled = [pltpu.roll(part, wide - PATCH, 1) for part in parts]
        done = []
        for index, part in enumerate(parts):
            if index % count == count - 1:
                following = jnp.where(lane < wide - PATCH, rolled[index], 0.0)
            else:
                following = jnp.where(lane < wide - PATCH, rolled[index], rolled[index + 1])
            value = part + sign * following
            value = jnp.where(krow == 0, value + value[HALF : HALF + 1] + value[HALF + 1 : HALF + 2], value)
            value = jnp.where(dc, 0.0, value)
            done.append(value)
        return done

    def groups(offset):
        fine_parts = [
            fine[KP * g : KP * (g + 1), offset * wide : (offset + 1) * wide]
            for g in range(fine_rows * tiles)
        ]
        coarse_parts = [
            jnp.concatenate(
                [
                    coarse[KP * g : KP * (g + 1), offset * LANES : (offset + 1) * LANES],
                    coarse[KP * (g + 1) : KP * (g + 2), offset * LANES : (offset + 1) * LANES],
                ],
                axis=1,
            )
            for g in range(0, coarse_rows * tiles, 2)
        ]
        return finish(fine_parts, fine_rows) + finish(coarse_parts, coarse_rows)

    return groups(0), groups(1)


def block_transpose(value):
    row = lax.broadcasted_iota(jnp.int32, value.shape, 0) % 4
    block = lax.broadcasted_iota(jnp.int32, value.shape, 1) // WINDOW
    rows = value.shape[0]
    moved = pltpu.roll(value, 2 * WINDOW, 1)
    other = jnp.where(row < 2, pltpu.roll(moved, rows - 2, 0), pltpu.roll(moved, 2, 0))
    value = jnp.where((row // 2) == (block // 2), value, other)
    right = pltpu.roll(pltpu.roll(value, WINDOW, 1), rows - 1, 0)
    left = pltpu.roll(pltpu.roll(value, LANES - WINDOW, 1), 1, 0)
    other = jnp.where(row % 2 == 0, right, left)
    return jnp.where((row % 2) == (block % 2), value, other)


def compute(const_count, *refs):
    pixels_ref, fine_mask_ref, coarse_mask_ref = refs[:3]
    sources = refs[3 : 3 + const_count]
    maps_ref = refs[3 + const_count]
    own_ref, near_ref, far_ref, rim_ref, real_ref, imag_ref, sums_ref = refs[4 + const_count : 11 + const_count]
    held = refs[11 + const_count : 11 + 2 * const_count]
    own_sem, const_sem, send_sem, recv_sem = refs[11 + 2 * const_count :]
    sec, strip = lax.axis_index("sec"), lax.axis_index("strip")
    secs, strips = lax.axis_size("sec"), lax.axis_size("strip")

    own_copy = pltpu.make_async_copy(pixels_ref.at[0], own_ref, own_sem)
    own_copy.start()
    const_copies = [
        pltpu.make_async_copy(source, target, const_sem.at[index])
        for index, (source, target) in enumerate(zip(sources, held))
    ]
    for copy in const_copies:
        copy.start()

    barrier = pltpu.get_barrier_semaphore()

    def greet(condition, device):
        @pl.when(condition)
        def _():
            pl.semaphore_signal(barrier, inc=1, device_id=device, device_id_type=MESH)

    greet(sec + 1 < secs, {"sec": sec + 1})
    greet(strip + 1 < strips, {"strip": strip + 1})
    targets = lax.min(sec, 1) + lax.min(strip, 1)

    @pl.when(targets >= 1)
    def _():
        pl.semaphore_wait(barrier, targets)

    piece = pixels_ref.shape[1] // CHUNKS

    def remote(source, target, flow, chunk, device):
        rows = pl.ds(piece * chunk, piece)
        return pltpu.make_async_remote_copy(
            src_ref=source.at[rows],
            dst_ref=target.at[rows],
            send_sem=send_sem.at[flow, chunk],
            recv_sem=recv_sem.at[flow, chunk],
            device_id=device,
            device_id_type=MESH,
        )

    above, before = {"strip": strip - 1}, {"sec": sec - 1}
    rim_copies = [
        [remote(source, rim_ref.at[index], index, c, above) for c in range(CHUNKS)]
        for index, source in enumerate((pixels_ref.at[0], near_ref, far_ref))
    ]
    near_copies = [remote(pixels_ref.at[0], near_ref, 3, c, before) for c in range(CHUNKS)]
    far_copies = [remote(near_ref, far_ref, 4, c, before) for c in range(CHUNKS)]
    up = strip >= 1
    below = strip + 1 < strips
    has_near, has_far = sec + 1 < secs, sec + 2 < secs

    def each(condition, copies, method):
        @pl.when(condition)
        def _():
            for copy in copies:
                getattr(copy, method)()

    for c in range(CHUNKS):
        pl.when(up)(rim_copies[0][c].start)
        pl.when(sec >= 1)(near_copies[c].start)

    def fill(condition, ref, *index):
        @pl.when(condition)
        def _():
            ref[index if index else ...] = jnp.zeros(ref.shape[len(index) :], ref.dtype)

    for d in range(3):
        fill(jnp.logical_not(below & (sec + d < secs)), rim_ref, d)
    fill(sec + 1 >= secs, near_ref)
    fill(sec + 2 >= secs, far_ref)
    sums_ref[...] = jnp.zeros_like(sums_ref)

    fine_rows, fine_cols = fine_mask_ref.shape[1:]
    coarse_rows, coarse_cols = coarse_mask_ref.shape[1:]
    count = (fine_rows * fine_cols + coarse_rows * coarse_cols) // 4
    (
        first_ref,
        fine_high_ref,
        fine_low_ref,
        coarse_high_ref,
        coarse_low_ref,
        inverse_high_ref,
        inverse_low_ref,
        last_ref,
        energy_ref,
        weight_ref,
    ) = held

    def spread(mask, cols):
        source = lax.broadcasted_iota(jnp.int32, (cols, cols * WINDOW), 0)
        target = lax.broadcasted_iota(jnp.int32, (cols, cols * WINDOW), 1) // WINDOW
        picks = jnp.where(source == target, 1.0, 0.0).astype(BF16)
        return matmul(mask.astype(F32).astype(BF16), picks)

    fine_mask = spread(fine_mask_ref[0], fine_cols)
    coarse_mask = spread(coarse_mask_ref[0], coarse_cols)
    masks = [
        m[r : r + 1, LANES * t : LANES * (t + 1)]
        for m in (fine_mask, coarse_mask)
        for r in range(m.shape[0])
        for t in range(m.shape[1] // LANES)
    ]
    scales = []

    def analyse(section, main_ref):
        each(below & (sec + section < secs), rim_copies[section], "wait_recv")
        weight = jnp.concatenate([weight_ref[...]] * 2, axis=1)
        real, imag = section_spectra(
            jnp.concatenate([main_ref[...], rim_ref[section]], axis=0),
            first_ref[...],
            (fine_high_ref[...], fine_low_ref[...]),
            (coarse_high_ref[...], coarse_low_ref[...]),
            fine_rows,
            coarse_rows,
        )
        for g in range(count):
            real_ref[section, KP * g : KP * (g + 1)] = real[g]
            imag_ref[section, KP * g : KP * (g + 1)] = imag[g]
            power = weight * (real[g] * real[g] + imag[g] * imag[g])
            sums_ref[section, g : g + 1] = jnp.sum(power, axis=0, keepdims=True)
        total = jnp.dot(
            sums_ref[section], energy_ref[...], preferred_element_type=F32, precision=lax.Precision.HIGHEST
        )
        scales.append(1.0 / jnp.sqrt(total * (1.0 / float(PATCH) ** 4) + 1e-05))

    def correlate(d):
        cross_real = real_ref[0] * real_ref[d] + imag_ref[0] * imag_ref[d]
        cross_imag = real_ref[0] * imag_ref[d] - imag_ref[0] * real_ref[d]
        cross = jnp.concatenate([cross_real.astype(BF16), cross_imag.astype(BF16)], axis=1)
        rows = matmul(cross, inverse_high_ref[...]) + matmul(cross, inverse_low_ref[...])
        stacked = []
        for g in range(count):
            part = rows[KP * g : KP * (g + 1)]
            stacked.append(jnp.concatenate([part[:, :LANES], part[:, LANES:]], axis=0))
        high, low = split_value(jnp.concatenate(stacked, axis=1))
        maps = matmul(last_ref[...], jnp.concatenate([high, low, high], axis=0))
        for g in range(count):
            scale = scales[0][g : g + 1] * scales[d][g : g + 1] * masks[g] * (1.0 / float(PATCH) ** 3)
            maps_ref[d - 1, g] = block_transpose(maps[:, LANES * g : LANES * (g + 1)] * scale)

    @pl.when(has_near)
    def _():
        for c in range(CHUNKS):
            near_copies[c].wait_recv()
            pl.when(up)(rim_copies[1][c].start)
            pl.when(sec >= 1)(far_copies[c].start)

    own_copy.wait()
    for copy in const_copies:
        copy.wait()
    analyse(0, own_ref)

    @pl.when(has_far)
    def _():
        for c in range(CHUNKS):
            far_copies[c].wait_recv()
            pl.when(up)(rim_copies[2][c].start)

    analyse(1, near_ref)
    correlate(1)
    analyse(2, far_ref)
    correlate(2)
    each(sec >= 1, near_copies, "wait_send")
    each(has_near & (sec >= 1), far_copies, "wait_send")
    each(up, rim_copies[0], "wait_send")
    each(has_near & up, rim_copies[1], "wait_send")
    each(has_far & up, rim_copies[2], "wait_send")


def arrange(maps_ref, fine_out_ref, coarse_out_ref):
    fine_rows, fine_cols = fine_out_ref.shape[2:4]
    coarse_rows, coarse_cols = coarse_out_ref.shape[2:4]
    fine_groups = fine_rows * fine_cols // 4
    count = fine_groups + coarse_rows * coarse_cols // 4
    for d in range(1):
        for g in range(count):
            value = maps_ref[d, g]
            if g < fine_groups:
                ref, local_g, cols = fine_out_ref, g, fine_cols
            else:
                ref, local_g, cols = coarse_out_ref, g - fine_groups, coarse_cols
            i, j = divmod(4 * local_g, cols)
            for q in range(WINDOW // 4):
                ref[0, d, i, j : j + 4, LANES * q : LANES * (q + 1)] = value[4 * q : 4 * (q + 1)]


def local(sections, mask_fine, mask_coarse):
    strip_rows, width = sections.shape[1:]
    consts = [jnp.asarray(t) for t in tables(strip_rows)]
    fine_rows, fine_cols = mask_fine.shape[1:]
    coarse_rows, coarse_cols = mask_coarse.shape[1:]
    count = (fine_rows * fine_cols + coarse_rows * coarse_cols) // 4
    vmem = pl.BlockSpec(memory_space=pltpu.VMEM)
    anywhere = pl.BlockSpec(memory_space=pl.ANY)
    flat = WINDOW * WINDOW
    maps = pl.pallas_call(
        functools.partial(compute, len(consts)),
        out_shape=jax.ShapeDtypeStruct((2, count, WINDOW, LANES), F32),
        in_specs=[anywhere, vmem, vmem] + [anywhere] * len(consts),
        out_specs=vmem,
        scratch_shapes=[
            pltpu.VMEM((strip_rows, width), BF16),
            pltpu.VMEM((strip_rows, width), BF16),
            pltpu.VMEM((strip_rows, width), BF16),
            pltpu.VMEM((3, strip_rows, width), BF16),
            pltpu.VMEM((3, KP * count, 2 * LANES), F32),
            pltpu.VMEM((3, KP * count, 2 * LANES), F32),
            pltpu.VMEM((3, -(-count // 8) * 8, 2 * LANES), F32),
            *[pltpu.VMEM(c.shape, c.dtype) for c in consts],
            pltpu.SemaphoreType.DMA,
            pltpu.SemaphoreType.DMA((len(consts),)),
            pltpu.SemaphoreType.DMA((5, CHUNKS)),
            pltpu.SemaphoreType.DMA((5, CHUNKS)),
        ],
        compiler_params=pltpu.CompilerParams(collective_id=0, has_side_effects=True),
    )(sections, mask_fine, mask_coarse, *consts)
    return pl.pallas_call(
        arrange,
        out_shape=(
            jax.ShapeDtypeStruct((1, 2, fine_rows, fine_cols, flat), F32),
            jax.ShapeDtypeStruct((1, 2, coarse_rows, coarse_cols, flat), F32),
        ),
        grid=(2,),
        in_specs=[pl.BlockSpec((1, count, WINDOW, LANES), lambda d: (d, 0, 0, 0))],
        out_specs=(
            pl.BlockSpec((1, 1, fine_rows, fine_cols, flat), lambda d: (0, d, 0, 0, 0)),
            pl.BlockSpec((1, 1, coarse_rows, coarse_cols, flat), lambda d: (0, d, 0, 0, 0)),
        ),
    )(maps)


def solution(mesh):
    in_specs = (
        P("sec", "strip", "groups"),
        P("sec", "strip", "groups"),
        P("sec", "strip", "groups"),
    )
    out_specs = (P("sec", None, "strip", "groups", None), P("sec", None, "strip", "groups", None))
    return jax.shard_map(local, mesh=mesh, in_specs=in_specs, out_specs=out_specs, check_vma=False)
```

profile of v0, /device:TPU:1, one launch (start us, length us, event | category | flops | bytes accessed | tf_op | source)
XLA Modules:
  0.0 18.0 jit_solution(16734327367046390080)
XLA Ops:
  0.6 15.7 %shard_map.140.maps_ref = f32[2,10,32,128]{3,2,1,0:T(8,128)} custom-call(bf16[1,64,512]{2,1,0:T(8,128)(2,1)} %refs_0_.1, s32[1,2,16]{2,1,0:T(2,128)} %refs_1_.1, s32[1,1,8]{2,1,0:T(1,128)} %refs_2_.1, bf16[240,256]{1,0:T(8,128)(2,1)} %constant.20.clone.refs_3_, bf16[256,512]{1,0:T(8,128)(2,1)} %constant.21.clone.refs_4_, ...), custom_call_target="tpu_custom_call" | custom-call | tf_op jit(solution)/shard_map/pallas_call | solution.py:383
  16.3 1.7 %shard_map.141 = (f32[1,2,2,16,1024]{4,3,2,1,0:T(8,128)}, f32[1,2,1,8,1024]{4,3,2,1,0:T(8,128)}) custom-call(f32[2,10,32,128]{3,2,1,0:T(8,128)} %shard_map.140.maps_ref), custom_call_target="tpu_custom_call" | custom-call | tf_op jit(solution)/shard_map/pallas_call | solution.py:404
where the time goes:
time: 18.2 us; the launch traced here: 18 us
  Pallas kernels  17.4 us (96%)
  between operations  0.64 us (4%)
    pallas_call x1, Pallas kernels, local(): pl.pallas_call(functools.partial(compute, len(consts)), out_shape=jax.Sha...  15.7 us
    pallas_call x1, Pallas kernels, local(): pl.pallas_call(arrange, out_shape=(jax.ShapeDtypeStruct((1, 2, fine_rows,...  1.69 us

commit v1 on v0

--- a/solution.py
+++ b/solution.py
@@ -13,7 +13,8 @@
 WINDOW = 32
 HALF = PATCH // 2 + 1
 KP = 40
-CHUNKS = 4
+CHUNKS = 2
+GRANT = 48 * 1024 * 1024
 LANES = 128
 F32 = jnp.float32
 BF16 = jnp.bfloat16
@@ -181,14 +182,29 @@
 def compute(const_count, *refs):
     pixels_ref, fine_mask_ref, coarse_mask_ref = refs[:3]
     sources = refs[3 : 3 + const_count]
-    maps_ref = refs[3 + const_count]
-    own_ref, near_ref, far_ref, rim_ref, real_ref, imag_ref, sums_ref = refs[4 + const_count : 11 + const_count]
+    fine_out_ref, coarse_out_ref = refs[3 + const_count : 5 + const_count]
+    main_ref, rim_ref, real_ref, imag_ref, sums_ref, scale_ref = refs[5 + const_count : 11 + const_count]
     held = refs[11 + const_count : 11 + 2 * const_count]
-    own_sem, const_sem, send_sem, recv_sem = refs[11 + 2 * const_count :]
+    own_sem, const_sem, send_sem, main_sem, rim_sem = refs[11 + 2 * const_count :]
     sec, strip = lax.axis_index("sec"), lax.axis_index("strip")
     secs, strips = lax.axis_size("sec"), lax.axis_size("strip")
-
-    own_copy = pltpu.make_async_copy(pixels_ref.at[0], own_ref, own_sem)
+    even, odd = strip % 2 == 0, strip % 2 == 1
+    below = strip + 1 < strips
+    has_near, has_far = sec + 1 < secs, sec + 2 < secs
+
+    barrier = pltpu.get_barrier_semaphore()
+
+    def greet(condition, device):
+        @pl.when(condition)
+        def _():
+            pl.semaphore_signal(barrier, inc=1, device_id=device, device_id_type=MESH)
+
+    greet(even & has_far, {"sec": sec + 2})
+    greet(odd & has_near & below, {"sec": sec + 1, "strip": strip + 1})
+    greet(has_near, {"sec": sec + 1})
+    greet(below, {"strip": strip + 1})
+
+    own_copy = pltpu.make_async_copy(pixels_ref.at[0], main_ref.at[0], own_sem)
     own_copy.start()
     const_copies = [
         pltpu.make_async_copy(source, target, const_sem.at[index])
@@ -197,44 +213,41 @@
     for copy in const_copies:
         copy.start()
 
-    barrier = pltpu.get_barrier_semaphore()
-
-    def greet(condition, device):
-        @pl.when(condition)
-        def _():
-            pl.semaphore_signal(barrier, inc=1, device_id=device, device_id_type=MESH)
-
-    greet(sec + 1 < secs, {"sec": sec + 1})
-    greet(strip + 1 < strips, {"strip": strip + 1})
-    targets = lax.min(sec, 1) + lax.min(strip, 1)
+    diagonal = even & (sec >= 1) & (strip >= 1)
+    routed = even & (sec >= 2)
+    one = lambda condition: jnp.where(condition, 1, 0)
+    targets = one(sec >= 1) + one(strip >= 1) + one(diagonal) + one(routed)
 
     @pl.when(targets >= 1)
     def _():
         pl.semaphore_wait(barrier, targets)
 
-    piece = pixels_ref.shape[1] // CHUNKS
-
-    def remote(source, target, flow, chunk, device):
-        rows = pl.ds(piece * chunk, piece)
-        return pltpu.make_async_remote_copy(
-            src_ref=source.at[rows],
-            dst_ref=target.at[rows],
-            send_sem=send_sem.at[flow, chunk],
-            recv_sem=recv_sem.at[flow, chunk],
-            device_id=device,
-            device_id_type=MESH,
-        )
-
+    piece = pixels_ref.shape[2] // CHUNKS
+
+    def remote(flow, source, target, sems, section, device):
+        def chunk(c):
+            columns = (slice(None), pl.ds(piece * c, piece))
+            return pltpu.make_async_remote_copy(
+                src_ref=source.at[columns],
+                dst_ref=target.at[section].at[columns],
+                send_sem=send_sem.at[flow, c],
+                recv_sem=sems.at[section, c],
+                device_id=device,
+                device_id_type=MESH,
+            )
+
+        return [chunk(c) for c in range(CHUNKS)]
+
+    own = pixels_ref.at[0]
     above, before = {"strip": strip - 1}, {"sec": sec - 1}
-    rim_copies = [
-        [remote(source, rim_ref.at[index], index, c, above) for c in range(CHUNKS)]
-        for index, source in enumerate((pixels_ref.at[0], near_ref, far_ref))
-    ]
-    near_copies = [remote(pixels_ref.at[0], near_ref, 3, c, before) for c in range(CHUNKS)]
-    far_copies = [remote(near_ref, far_ref, 4, c, before) for c in range(CHUNKS)]
-    up = strip >= 1
-    below = strip + 1 < strips
-    has_near, has_far = sec + 1 < secs, sec + 2 < secs
+    near_send = remote(0, own, main_ref, main_sem, 1, before)
+    rim_send = remote(1, own, rim_ref, rim_sem, 0, above)
+    diagonal_send = remote(2, own, rim_ref, rim_sem, 1, {"sec": sec - 1, "strip": strip - 1})
+    routed_send = remote(3, own, main_ref, main_sem, 2, {"sec": sec - 2})
+    far_relay = remote(4, main_ref.at[1], main_ref, main_sem, 2, before)
+    near_rim_relay = remote(5, main_ref.at[1], rim_ref, rim_sem, 1, above)
+    far_rim_relay = remote(6, rim_ref.at[1], rim_ref, rim_sem, 2, before)
+    far_rim_across = remote(7, main_ref.at[2], rim_ref, rim_sem, 2, above)
 
     def each(condition, copies, method):
         @pl.when(condition)
@@ -242,24 +255,21 @@
             for copy in copies:
                 getattr(copy, method)()
 
-    for c in range(CHUNKS):
-        pl.when(up)(rim_copies[0][c].start)
-        pl.when(sec >= 1)(near_copies[c].start)
-
-    def fill(condition, ref, *index):
-        @pl.when(condition)
-        def _():
-            ref[index if index else ...] = jnp.zeros(ref.shape[len(index) :], ref.dtype)
-
-    for d in range(3):
-        fill(jnp.logical_not(below & (sec + d < secs)), rim_ref, d)
-    fill(sec + 1 >= secs, near_ref)
-    fill(sec + 2 >= secs, far_ref)
+    each(diagonal, diagonal_send, "start")
+    each(routed, routed_send, "start")
+    each(sec >= 1, near_send, "start")
+    each(strip >= 1, rim_send, "start")
+
+    @pl.when(jnp.logical_not(below))
+    def _():
+        rim_ref[...] = jnp.zeros_like(rim_ref)
+
     sums_ref[...] = jnp.zeros_like(sums_ref)
 
     fine_rows, fine_cols = fine_mask_ref.shape[1:]
     coarse_rows, coarse_cols = coarse_mask_ref.shape[1:]
-    count = (fine_rows * fine_cols + coarse_rows * coarse_cols) // 4
+    fine_groups = fine_rows * fine_cols // 4
+    count = fine_groups + coarse_rows * coarse_cols // 4
     (
         first_ref,
         fine_high_ref,
@@ -287,13 +297,11 @@
         for r in range(m.shape[0])
         for t in range(m.shape[1] // LANES)
     ]
-    scales = []
-
-    def analyse(section, main_ref):
-        each(below & (sec + section < secs), rim_copies[section], "wait_recv")
+
+    def analyse(section):
         weight = jnp.concatenate([weight_ref[...]] * 2, axis=1)
         real, imag = section_spectra(
-            jnp.concatenate([main_ref[...], rim_ref[section]], axis=0),
+            jnp.concatenate([main_ref[section], rim_ref[section]], axis=0),
             first_ref[...],
             (fine_high_ref[...], fine_low_ref[...]),
             (coarse_high_ref[...], coarse_low_ref[...]),
@@ -308,7 +316,7 @@
         total = jnp.dot(
             sums_ref[section], energy_ref[...], preferred_element_type=F32, precision=lax.Precision.HIGHEST
         )
-        scales.append(1.0 / jnp.sqrt(total * (1.0 / float(PATCH) ** 4) + 1e-05))
+        scale_ref[section] = 1.0 / jnp.sqrt(total * (1.0 / float(PATCH) ** 4) + 1e-05)
 
     def correlate(d):
         cross_real = real_ref[0] * real_ref[d] + imag_ref[0] * imag_ref[d]
@@ -321,54 +329,81 @@
             stacked.append(jnp.concatenate([part[:, :LANES], part[:, LANES:]], axis=0))
         high, low = split_value(jnp.concatenate(stacked, axis=1))
         maps = matmul(last_ref[...], jnp.concatenate([high, low, high], axis=0))
+        both = scale_ref[0] * scale_ref[d] * (1.0 / float(PATCH) ** 3)
         for g in range(count):
-            scale = scales[0][g : g + 1] * scales[d][g : g + 1] * masks[g] * (1.0 / float(PATCH) ** 3)
-            maps_ref[d - 1, g] = block_transpose(maps[:, LANES * g : LANES * (g + 1)] * scale)
-
-    @pl.when(has_near)
-    def _():
-        for c in range(CHUNKS):
-            near_copies[c].wait_recv()
-            pl.when(up)(rim_copies[1][c].start)
-            pl.when(sec >= 1)(far_copies[c].start)
-
-    own_copy.wait()
-    for copy in const_copies:
-        copy.wait()
-    analyse(0, own_ref)
-
-    @pl.when(has_far)
-    def _():
-        for c in range(CHUNKS):
-            far_copies[c].wait_recv()
-            pl.when(up)(rim_copies[2][c].start)
-
-    analyse(1, near_ref)
-    correlate(1)
-    analyse(2, far_ref)
-    correlate(2)
-    each(sec >= 1, near_copies, "wait_send")
-    each(has_near & (sec >= 1), far_copies, "wait_send")
-    each(up, rim_copies[0], "wait_send")
-    each(has_near & up, rim_copies[1], "wait_send")
-    each(has_far & up, rim_copies[2], "wait_send")
-
-
-def arrange(maps_ref, fine_out_ref, coarse_out_ref):
-    fine_rows, fine_cols = fine_out_ref.shape[2:4]
-    coarse_rows, coarse_cols = coarse_out_ref.shape[2:4]
-    fine_groups = fine_rows * fine_cols // 4
-    count = fine_groups + coarse_rows * coarse_cols // 4
-    for d in range(1):
-        for g in range(count):
-            value = maps_ref[d, g]
+            scale = both[g : g + 1] * masks[g]
+            value = block_transpose(maps[:, LANES * g : LANES * (g + 1)] * scale)
             if g < fine_groups:
                 ref, local_g, cols = fine_out_ref, g, fine_cols
             else:
                 ref, local_g, cols = coarse_out_ref, g - fine_groups, coarse_cols
             i, j = divmod(4 * local_g, cols)
             for q in range(WINDOW // 4):
-                ref[0, d, i, j : j + 4, LANES * q : LANES * (q + 1)] = value[4 * q : 4 * (q + 1)]
+                ref[0, d - 1, i, j : j + 4, LANES * q : LANES * (q + 1)] = value[4 * q : 4 * (q + 1)]
+
+    def clear(d):
+        for ref in (fine_out_ref, coarse_out_ref):
+            ref[0, d - 1] = jnp.zeros(ref.shape[2:], F32)
+
+    own_copy.wait()
+    for copy in const_copies:
+        copy.wait()
+    each(below, rim_send, "wait_recv")
+    analyse(0)
+
+    @pl.when(has_near)
+    def _():
+        for c in range(CHUNKS):
+            near_send[c].wait_recv()
+            pl.when(odd & (sec >= 1))(far_relay[c].start)
+            pl.when(odd)(near_rim_relay[c].start)
+
+        @pl.when(below)
+        def _():
+            for c in range(CHUNKS):
+                near_rim_relay[c].wait_recv()
+                pl.when(odd & (sec >= 1))(far_rim_relay[c].start)
+
+        analyse(1)
+
+    @pl.when(has_far)
+    def _():
+        for c in range(CHUNKS):
+            far_relay[c].wait_recv()
+            pl.when(odd)(far_rim_across[c].start)
+
+    @pl.when(has_near)
+    def _():
+        correlate(1)
+
+    @pl.when(has_far)
+    def _():
+        each(below, far_rim_relay, "wait_recv")
+        analyse(2)
+        correlate(2)
+
+    pl.when(jnp.logical_not(has_near))(lambda: clear(1))
+    pl.when(jnp.logical_not(has_far))(lambda: clear(2))
+    each(sec >= 1, near_send, "wait_send")
+    each(strip >= 1, rim_send, "wait_send")
+    each(diagonal, diagonal_send, "wait_send")
+    each(routed, routed_send, "wait_send")
+    each(odd & has_near & (sec >= 1), far_relay, "wait_send")
+    each(odd & has_near, near_rim_relay, "wait_send")
+    each(odd & has_near & below & (sec >= 1), far_rim_relay, "wait_send")
+    each(odd & has_far, far_rim_across, "wait_send")
+
+
+def deliver(fine_ref, coarse_ref, fine_out_ref, coarse_out_ref, sem):
+    copies = [
+        pltpu.make_async_copy(source.at[0, d], target.at[0, d], sem.at[index, d])
+        for index, (source, target) in enumerate(((fine_ref, fine_out_ref), (coarse_ref, coarse_out_ref)))
+        for d in range(2)
+    ]
+    for copy in copies:
+        copy.start()
+    for copy in copies:
+        copy.wait()
 
 
 def local(sections, mask_fine, mask_coarse):
@@ -380,40 +415,41 @@
     vmem = pl.BlockSpec(memory_space=pltpu.VMEM)
     anywhere = pl.BlockSpec(memory_space=pl.ANY)
     flat = WINDOW * WINDOW
+    sums = -(-count // 8) * 8
+    shapes = (
+        jax.ShapeDtypeStruct((1, 2, fine_rows, fine_cols, flat), F32),
+        jax.ShapeDtypeStruct((1, 2, coarse_rows, coarse_cols, flat), F32),
+    )
+    operands = [pltpu.with_memory_space_constraint(t, pltpu.HBM) for t in (sections, mask_fine, mask_coarse, *consts)]
     maps = pl.pallas_call(
         functools.partial(compute, len(consts)),
-        out_shape=jax.ShapeDtypeStruct((2, count, WINDOW, LANES), F32),
+        out_shape=shapes,
         in_specs=[anywhere, vmem, vmem] + [anywhere] * len(consts),
-        out_specs=vmem,
+        out_specs=(vmem, vmem),
         scratch_shapes=[
-            pltpu.VMEM((strip_rows, width), BF16),
-            pltpu.VMEM((strip_rows, width), BF16),
-            pltpu.VMEM((strip_rows, width), BF16),
+            pltpu.VMEM((3, strip_rows, width), BF16),
             pltpu.VMEM((3, strip_rows, width), BF16),
             pltpu.VMEM((3, KP * count, 2 * LANES), F32),
             pltpu.VMEM((3, KP * count, 2 * LANES), F32),
-            pltpu.VMEM((3, -(-count // 8) * 8, 2 * LANES), F32),
+            pltpu.VMEM((3, sums, 2 * LANES), F32),
+            pltpu.VMEM((3, sums, LANES), F32),
             *[pltpu.VMEM(c.shape, c.dtype) for c in consts],
             pltpu.SemaphoreType.DMA,
             pltpu.SemaphoreType.DMA((len(consts),)),
-            pltpu.SemaphoreType.DMA((5, CHUNKS)),
-            pltpu.SemaphoreType.DMA((5, CHUNKS)),
+            pltpu.SemaphoreType.DMA((8, CHUNKS)),
+            pltpu.SemaphoreType.DMA((3, CHUNKS)),
+            pltpu.SemaphoreType.DMA((3, CHUNKS)),
         ],
-        compiler_params=pltpu.CompilerParams(collective_id=0, has_side_effects=True),
-    )(sections, mask_fine, mask_coarse, *consts)
+        compiler_params=pltpu.CompilerParams(collective_id=0, has_side_effects=True, vmem_limit_bytes=GRANT),
+    )(*operands)
     return pl.pallas_call(
-        arrange,
-        out_shape=(
-            jax.ShapeDtypeStruct((1, 2, fine_rows, fine_cols, flat), F32),
-            jax.ShapeDtypeStruct((1, 2, coarse_rows, coarse_cols, flat), F32),
-        ),
-        grid=(2,),
-        in_specs=[pl.BlockSpec((1, count, WINDOW, LANES), lambda d: (d, 0, 0, 0))],
-        out_specs=(
-            pl.BlockSpec((1, 1, fine_rows, fine_cols, flat), lambda d: (0, d, 0, 0, 0)),
-            pl.BlockSpec((1, 1, coarse_rows, coarse_cols, flat), lambda d: (0, d, 0, 0, 0)),
-        ),
-    )(maps)
+        deliver,
+        out_shape=shapes,
+        in_specs=[vmem, vmem],
+        out_specs=(anywhere, anywhere),
+        scratch_shapes=[pltpu.SemaphoreType.DMA((2, 2))],
+        compiler_params=pltpu.CompilerParams(vmem_limit_bytes=GRANT),
+    )(*maps)
 
 
 def solution(mesh):

time: 18.2 us -> 14.8 us (0.81)
  the two profiles are of different devices: /device:TPU:1 before, /device:TPU:0 now
where the time goes in v1:
time: 14.8 us; the launch traced here: 14.7 us
  Pallas kernels  14 us (95%)
  between operations  0.64 us (4%)
    pallas_call x1, Pallas kernels, local(): pl.pallas_call(functools.partial(compute, len(consts)), out_shape=shapes,...  13.3 us
    pallas_call x1, Pallas kernels, local(): pl.pallas_call(deliver, out_shape=shapes, in_specs=[vmem, vmem], out_spec...  0.75 us

profile of v1, /device:TPU:0, one launch (start us, length us, event | category | flops | bytes accessed | tf_op | source)
XLA Modules:
  0.0 14.7 jit_solution(17137412358359074085)
XLA Ops:
  0.6 13.3 %shard_map.140 = (f32[1,2,2,16,1024]{4,3,2,1,0:T(8,128)S(1)}, f32[1,2,1,8,1024]{4,3,2,1,0:T(8,128)S(1)}) custom-call(bf16[1,64,512]{2,1,0:T(8,128)(2,1)} %refs_0_.1, s32[1,2,16]{2,1,0:T(2,128)} %refs_1_.1, s32[1,1,8]{2,1,0:T(1,128)} %refs_2_.1, bf16[240,256]{1,0:T(8,128)(2,1)} %constant.20.clone.refs_3_, bf16[256,512]{1,0:T(8,128)(2,1)} %constant.21.clone.refs_4_, ...), custom_call_target="tpu_custom_call" | custom-call | tf_op jit(solution)/shard_map/pallas_call | solution.py:424
  13.9 0.7 %shard_map.141 = (f32[1,2,2,16,1024]{4,3,2,1,0:T(8,128)}, f32[1,2,1,8,1024]{4,3,2,1,0:T(8,128)}) custom-call(f32[1,2,2,16,1024]{4,3,2,1,0:T(8,128)S(1)} %get-tuple-element.4.fine_ref, f32[1,2,1,8,1024]{4,3,2,1,0:T(8,128)S(1)} %get-tuple-element.5.coarse_ref), custom_call_target="tpu_custom_call" | custom-call | tf_op jit(solution)/shard_map/pallas_call | solution.py:445

commit v2 on v1

--- a/solution.py
+++ b/solution.py
@@ -14,6 +14,7 @@
 HALF = PATCH // 2 + 1
 KP = 40
 CHUNKS = 2
+TABLE_SCALE = 1.869
 GRANT = 48 * 1024 * 1024
 LANES = 128
 F32 = jnp.float32
@@ -36,9 +37,24 @@
     return np.kron(np.eye(count), block)
 
 
+def rounded(table):
+    scaled = np.asarray(table, np.float64) * TABLE_SCALE
+    return scaled.astype(np.float32).astype(BF16)
+
+
+def table_gain():
+    c, _ = trig(np.arange(PATCH))
+    return float(c @ rounded(c).astype(np.float64) / (c @ c))
+
+
+def inner_rows(strip_rows):
+    return len([i for i in range(strip_rows // STRIDE) if STRIDE * i + PATCH <= strip_rows])
+
+
 def tables(strip_rows):
     fine_rows = strip_rows // STRIDE
     coarse_rows = strip_rows // (2 * STRIDE)
+    inner = inner_rows(strip_rows)
     height = strip_rows + PATCH
     k = np.arange(KP)[:, None]
     keep = (k < HALF).astype(np.float64)
@@ -53,8 +69,14 @@
         c, s = trig(k * xc)
         inside = ((xc >= 0) & (xc < PATCH)) * keep * 0.25
         units += [c * inside, -s * inside]
-    a_high, a_low = split(np.concatenate(units, axis=0))
-    first = np.concatenate([a_high, a_low], axis=1)
+
+    def first(parts, rows):
+        high, low = split(np.concatenate(parts, axis=0)[:, :rows])
+        return np.concatenate([high, low], axis=1)
+
+    firsts = [first(units[2 * inner :], height)]
+    if inner:
+        firsts.insert(0, first(units[: 2 * inner], strip_rows))
 
     freq = np.arange(PATCH)[None, :]
     y = np.arange(STRIDE)[:, None]
@@ -62,7 +84,7 @@
 
     def second(c, s, count):
         c, s = block_diagonal(c, count), block_diagonal(s, count)
-        return split(np.block([[c, -s], [s, c]]))
+        return rounded(np.block([[c, -s], [s, c]]))
 
     fine_w = second(c, s, LANES // STRIDE)
     coarse_w = second(np.repeat(c, 2, axis=0), np.repeat(s, 2, axis=0), LANES // (2 * STRIDE))
@@ -70,7 +92,7 @@
     shift = np.arange(WINDOW) - WINDOW // 2
     c, s = trig(np.arange(PATCH)[:, None] * shift[None, :])
     c, s = block_diagonal(c, 4), block_diagonal(s, 4)
-    inverse = split(np.block([[c, s], [-s, c]]))
+    inverse = rounded(np.block([[c, s], [-s, c]]))
 
     weight = np.where((k == 0) | (k == PATCH // 2), 1.0, 2.0) * keep
     c, s = trig(shift[:, None] * np.arange(KP)[None, :])
@@ -78,13 +100,13 @@
     last = np.concatenate([last_high, last_high, last_low], axis=1)
     energy = np.kron(np.eye(4), np.ones((PATCH, WINDOW)))
     return [
-        first,
-        *fine_w,
-        *coarse_w,
-        *inverse,
+        fine_w,
+        coarse_w,
+        inverse,
         last,
-        np.asarray(energy, np.float32),
+        np.asarray(energy, np.float32).astype(BF16),
         np.asarray(np.broadcast_to(weight, (KP, LANES)), np.float32),
+        *firsts,
     ]
 
 
@@ -120,11 +142,10 @@
 
     def transform(parts, weights):
         high, low = split_value(jnp.concatenate(parts, axis=0))
-        w_high, w_low = weights
-        return matmul(high, w_high) + matmul(low, w_high) + matmul(high, w_low)
-
-    fine = transform(fine_in, fine_w)
-    coarse = transform(coarse_in, coarse_w)
+        return matmul(high, weights) + matmul(low, weights)
+
+    fine = transform(fine_in, fine_w) if fine_rows else None
+    coarse = transform(coarse_in, coarse_w) if coarse_rows else None
     wide = 2 * LANES
     lane = lax.broadcasted_iota(jnp.int32, (KP, wide), 1)
     krow = lax.broadcasted_iota(jnp.int32, (KP, wide), 0)
@@ -161,7 +182,8 @@
             )
             for g in range(0, coarse_rows * tiles, 2)
         ]
-        return finish(fine_parts, fine_rows) + finish(coarse_parts, coarse_rows)
+        done = finish(fine_parts, fine_rows) if fine_rows else []
+        return done + (finish(coarse_parts, coarse_rows) if coarse_rows else [])
 
     return groups(0), groups(1)
 
@@ -183,9 +205,9 @@
     pixels_ref, fine_mask_ref, coarse_mask_ref = refs[:3]
     sources = refs[3 : 3 + const_count]
     fine_out_ref, coarse_out_ref = refs[3 + const_count : 5 + const_count]
-    main_ref, rim_ref, real_ref, imag_ref, sums_ref, scale_ref = refs[5 + const_count : 11 + const_count]
-    held = refs[11 + const_count : 11 + 2 * const_count]
-    own_sem, const_sem, send_sem, main_sem, rim_sem = refs[11 + 2 * const_count :]
+    main_ref, rim_ref, real_ref, imag_ref, scale_ref = refs[5 + const_count : 10 + const_count]
+    held = refs[10 + const_count : 10 + 2 * const_count]
+    own_sem, const_sem, send_sem, main_sem, rim_sem = refs[10 + 2 * const_count :]
     sec, strip = lax.axis_index("sec"), lax.axis_index("strip")
     secs, strips = lax.axis_size("sec"), lax.axis_size("strip")
     even, odd = strip % 2 == 0, strip % 2 == 1
@@ -255,33 +277,25 @@
             for copy in copies:
                 getattr(copy, method)()
 
+    each(strip >= 1, rim_send, "start")
     each(diagonal, diagonal_send, "start")
+    each(sec >= 1, near_send, "start")
     each(routed, routed_send, "start")
-    each(sec >= 1, near_send, "start")
-    each(strip >= 1, rim_send, "start")
 
     @pl.when(jnp.logical_not(below))
     def _():
         rim_ref[...] = jnp.zeros_like(rim_ref)
-
-    sums_ref[...] = jnp.zeros_like(sums_ref)
 
     fine_rows, fine_cols = fine_mask_ref.shape[1:]
     coarse_rows, coarse_cols = coarse_mask_ref.shape[1:]
     fine_groups = fine_rows * fine_cols // 4
     count = fine_groups + coarse_rows * coarse_cols // 4
-    (
-        first_ref,
-        fine_high_ref,
-        fine_low_ref,
-        coarse_high_ref,
-        coarse_low_ref,
-        inverse_high_ref,
-        inverse_low_ref,
-        last_ref,
-        energy_ref,
-        weight_ref,
-    ) = held
+    fine_w_ref, coarse_w_ref, inverse_ref, last_ref, energy_ref, weight_ref = held[:6]
+    first_refs = held[6:]
+    inner = inner_rows(pixels_ref.shape[1])
+    inner_groups = inner * fine_cols // 4
+    bounds = {"inner": (0, inner_groups), "outer": (inner_groups, count)}
+    gain = table_gain()
 
     def spread(mask, cols):
         source = lax.broadcasted_iota(jnp.int32, (cols, cols * WINDOW), 0)
@@ -298,41 +312,54 @@
         for t in range(m.shape[1] // LANES)
     ]
 
-    def analyse(section):
+    def analyse(section, part):
+        start, stop = bounds[part]
+        if start == stop:
+            return
         weight = jnp.concatenate([weight_ref[...]] * 2, axis=1)
-        real, imag = section_spectra(
-            jnp.concatenate([main_ref[section], rim_ref[section]], axis=0),
-            first_ref[...],
-            (fine_high_ref[...], fine_low_ref[...]),
-            (coarse_high_ref[...], coarse_low_ref[...]),
-            fine_rows,
-            coarse_rows,
-        )
-        for g in range(count):
-            real_ref[section, KP * g : KP * (g + 1)] = real[g]
-            imag_ref[section, KP * g : KP * (g + 1)] = imag[g]
-            power = weight * (real[g] * real[g] + imag[g] * imag[g])
-            sums_ref[section, g : g + 1] = jnp.sum(power, axis=0, keepdims=True)
-        total = jnp.dot(
-            sums_ref[section], energy_ref[...], preferred_element_type=F32, precision=lax.Precision.HIGHEST
-        )
-        scale_ref[section] = 1.0 / jnp.sqrt(total * (1.0 / float(PATCH) ** 4) + 1e-05)
-
-    def correlate(d):
-        cross_real = real_ref[0] * real_ref[d] + imag_ref[0] * imag_ref[d]
-        cross_imag = real_ref[0] * imag_ref[d] - imag_ref[0] * real_ref[d]
+        if part == "inner":
+            pixels, rows = main_ref[section], (inner, 0)
+        else:
+            pixels = jnp.concatenate([main_ref[section], rim_ref[section]], axis=0)
+            rows = (fine_rows - inner, coarse_rows)
+        first = first_refs[0 if part == "inner" else -1][...]
+        real, imag = section_spectra(pixels, first, fine_w_ref[...], coarse_w_ref[...], *rows)
+        sums = []
+        for g in range(start, stop):
+            re, im = real[g - start], imag[g - start]
+            real_ref[section, KP * g : KP * (g + 1)] = re
+            imag_ref[section, KP * g : KP * (g + 1)] = im
+            sums.append(jnp.sum(weight * (re * re + im * im), axis=0, keepdims=True))
+        sums = jnp.concatenate(sums, axis=0)
+        high, rest = split_value(sums)
+        low = (sums - high.astype(F32) - rest.astype(F32)).astype(BF16)
+        energy = energy_ref[...]
+        total = matmul(high, energy) + matmul(rest, energy) + matmul(low, energy)
+        scale = 1.0 / jnp.sqrt(total * (1.0 / (float(PATCH) ** 4 * gain * gain)) + 1e-05)
+        scale_ref[section, start:stop] = scale
+
+    def correlate(d, part):
+        start, stop = bounds[part]
+        if start == stop:
+            return
+        rows = slice(KP * start, KP * stop)
+        own_real, own_imag = real_ref[0, rows], imag_ref[0, rows]
+        other_real, other_imag = real_ref[d, rows], imag_ref[d, rows]
+        cross_real = own_real * other_real + own_imag * other_imag
+        cross_imag = own_real * other_imag - own_imag * other_real
         cross = jnp.concatenate([cross_real.astype(BF16), cross_imag.astype(BF16)], axis=1)
-        rows = matmul(cross, inverse_high_ref[...]) + matmul(cross, inverse_low_ref[...])
+        rows = matmul(cross, inverse_ref[...])
         stacked = []
-        for g in range(count):
-            part = rows[KP * g : KP * (g + 1)]
-            stacked.append(jnp.concatenate([part[:, :LANES], part[:, LANES:]], axis=0))
+        for g in range(stop - start):
+            piece = rows[KP * g : KP * (g + 1)]
+            stacked.append(jnp.concatenate([piece[:, :LANES], piece[:, LANES:]], axis=0))
         high, low = split_value(jnp.concatenate(stacked, axis=1))
         maps = matmul(last_ref[...], jnp.concatenate([high, low, high], axis=0))
-        both = scale_ref[0] * scale_ref[d] * (1.0 / float(PATCH) ** 3)
-        for g in range(count):
-            scale = both[g : g + 1] * masks[g]
-            value = block_transpose(maps[:, LANES * g : LANES * (g + 1)] * scale)
+        both = scale_ref[0, start:stop] * scale_ref[d, start:stop] * (1.0 / (float(PATCH) ** 3 * gain**3))
+        for g in range(start, stop):
+            at = g - start
+            scale = both[at : at + 1] * masks[g]
+            value = block_transpose(maps[:, LANES * at : LANES * (at + 1)] * scale)
             if g < fine_groups:
                 ref, local_g, cols = fine_out_ref, g, fine_cols
             else:
@@ -348,9 +375,7 @@
     own_copy.wait()
     for copy in const_copies:
         copy.wait()
-    each(below, rim_send, "wait_recv")
-    analyse(0)
-
+    analyse(0, "inner")
     @pl.when(has_near)
     def _():
         for c in range(CHUNKS):
@@ -358,13 +383,19 @@
             pl.when(odd & (sec >= 1))(far_relay[c].start)
             pl.when(odd)(near_rim_relay[c].start)
 
+    each(below, rim_send, "wait_recv")
+    analyse(0, "outer")
+
+    @pl.when(has_near)
+    def _():
         @pl.when(below)
         def _():
             for c in range(CHUNKS):
                 near_rim_relay[c].wait_recv()
                 pl.when(odd & (sec >= 1))(far_rim_relay[c].start)
 
-        analyse(1)
+        analyse(1, "inner")
+        analyse(1, "outer")
 
     @pl.when(has_far)
     def _():
@@ -374,13 +405,16 @@
 
     @pl.when(has_near)
     def _():
-        correlate(1)
+        correlate(1, "inner")
+        correlate(1, "outer")
 
     @pl.when(has_far)
     def _():
+        analyse(2, "inner")
+        correlate(2, "inner")
         each(below, far_rim_relay, "wait_recv")
-        analyse(2)
-        correlate(2)
+        analyse(2, "outer")
+        correlate(2, "outer")
 
     pl.when(jnp.logical_not(has_near))(lambda: clear(1))
     pl.when(jnp.logical_not(has_far))(lambda: clear(2))
@@ -415,7 +449,6 @@
     vmem = pl.BlockSpec(memory_space=pltpu.VMEM)
     anywhere = pl.BlockSpec(memory_space=pl.ANY)
     flat = WINDOW * WINDOW
-    sums = -(-count // 8) * 8
     shapes = (
         jax.ShapeDtypeStruct((1, 2, fine_rows, fine_cols, flat), F32),
         jax.ShapeDtypeStruct((1, 2, coarse_rows, coarse_cols, flat), F32),
@@ -431,8 +464,7 @@
             pltpu.VMEM((3, strip_rows, width), BF16),
             pltpu.VMEM((3, KP * count, 2 * LANES), F32),
             pltpu.VMEM((3, KP * count, 2 * LANES), F32),
-            pltpu.VMEM((3, sums, 2 * LANES), F32),
-            pltpu.VMEM((3, sums, LANES), F32),
+            pltpu.VMEM((3, count, LANES), F32),
             *[pltpu.VMEM(c.shape, c.dtype) for c in consts],
             pltpu.SemaphoreType.DMA,
             pltpu.SemaphoreType.DMA((len(consts),)),

time: 14.8 us -> 13.7 us (0.926)
  Pallas kernels: 14 us -> 12.9 us
    pallas_call x1, Pallas kernels: 13.3 us -> 12.2 us  [local(): pl.pallas_call(functools.partial(compute, len(consts)), out_shape=shapes,...]
where the time goes in v2:
time: 13.7 us; the launch traced here: 13.6 us
  Pallas kernels  12.9 us (94%)
  between operations  0.64 us (5%)
    pallas_call x1, Pallas kernels, local(): pl.pallas_call(functools.partial(compute, len(consts)), out_shape=shapes,...  12.2 us
    pallas_call x1, Pallas kernels, local(): pl.pallas_call(deliver, out_shape=shapes, in_specs=[vmem, vmem], out_spec...  0.75 us

profile of v2, /device:TPU:0, one launch (start us, length us, event | category | flops | bytes accessed | tf_op | source)
XLA Modules:
  0.0 13.6 jit_solution(14353772280656589715)
XLA Ops:
  0.6 12.2 %shard_map.122 = (f32[1,2,2,16,1024]{4,3,2,1,0:T(8,128)S(1)}, f32[1,2,1,8,1024]{4,3,2,1,0:T(8,128)S(1)}) custom-call(bf16[1,64,512]{2,1,0:T(8,128)(2,1)} %refs_0_.1, s32[1,2,16]{2,1,0:T(2,128)} %refs_1_.1, s32[1,1,8]{2,1,0:T(1,128)} %refs_2_.1, bf16[256,512]{1,0:T(8,128)(2,1)} %constant.16.clone.refs_3_, bf16[256,256]{1,0:T(8,128)(2,1)} %constant.17.clone.refs_4_, ...), custom_call_target="tpu_custom_call" | custom-call | tf_op jit(solution)/shard_map/pallas_call | solution.py:457
  12.8 0.7 %shard_map.123 = (f32[1,2,2,16,1024]{4,3,2,1,0:T(8,128)}, f32[1,2,1,8,1024]{4,3,2,1,0:T(8,128)}) custom-call(f32[1,2,2,16,1024]{4,3,2,1,0:T(8,128)S(1)} %get-tuple-element.4.fine_ref, f32[1,2,1,8,1024]{4,3,2,1,0:T(8,128)S(1)} %get-tuple-element.5.coarse_ref), custom_call_target="tpu_custom_call" | custom-call | tf_op jit(solution)/shard_map/pallas_call | solution.py:477

commit v3 on v2

--- a/solution.py
+++ b/solution.py
@@ -11,8 +11,7 @@
 PATCH = 64
 STRIDE = 32
 WINDOW = 32
-HALF = PATCH // 2 + 1
-KP = 40
+SLOTS = PATCH // 2
 CHUNKS = 2
 TABLE_SCALE = 1.869
 GRANT = 48 * 1024 * 1024
@@ -56,58 +55,68 @@
     coarse_rows = strip_rows // (2 * STRIDE)
     inner = inner_rows(strip_rows)
     height = strip_rows + PATCH
-    k = np.arange(KP)[:, None]
-    keep = (k < HALF).astype(np.float64)
+    k = np.concatenate([[PATCH // 2], np.arange(1, SLOTS)])[:, None]
     x = np.arange(height)[None, :]
-    units = []
+    units, sums = [], []
     for i in range(fine_rows):
+        inside = ((x >= STRIDE * i) & (x < STRIDE * i + PATCH)) * 1.0
         c, s = trig(k * (x - STRIDE * i))
-        inside = ((x >= STRIDE * i) & (x < STRIDE * i + PATCH)) * keep
-        units += [c * inside, -s * inside]
+        units.append(np.concatenate([c * inside, -s * inside]))
+        sums.append(np.repeat(inside, 8, axis=0))
     for i in range(coarse_rows):
         xc = x // 2 - STRIDE * i
+        inside = ((xc >= 0) & (xc < PATCH)) * 0.25
         c, s = trig(k * xc)
-        inside = ((xc >= 0) & (xc < PATCH)) * keep * 0.25
-        units += [c * inside, -s * inside]
-
-    def first(parts, rows):
-        high, low = split(np.concatenate(parts, axis=0)[:, :rows])
+        units.append(np.concatenate([c * inside, -s * inside]))
+        sums.append(np.repeat(inside, 8, axis=0))
+
+    def first(at, rows):
+        high, low = split(np.concatenate(units[at] + sums[at], axis=0)[:, :rows])
         return np.concatenate([high, low], axis=1)
 
-    firsts = [first(units[2 * inner :], height)]
+    firsts = [first(slice(inner, None), height)]
     if inner:
-        firsts.insert(0, first(units[: 2 * inner], strip_rows))
-
+        firsts.insert(0, first(slice(0, inner), strip_rows))
+
+    lane = np.arange(LANES)
+    half, quarter = LANES // 2, LANES // 4
+    middle = (lane >= quarter) & (lane < 3 * quarter)
+    windows = [
+        (lane % half, lane >= half),
+        (np.where(middle, lane - quarter, np.where(lane < quarter, lane + quarter, lane - 3 * quarter)), ~middle),
+        (lane % half, lane < half),
+        (np.where(lane < quarter, lane + quarter, np.where(middle, lane - quarter, lane - 3 * quarter)), middle),
+    ]
     freq = np.arange(PATCH)[None, :]
-    y = np.arange(STRIDE)[:, None]
-    c, s = trig(y * freq)
-
-    def second(c, s, count):
-        c, s = block_diagonal(c, count), block_diagonal(s, count)
-        return rounded(np.block([[c, -s], [s, c]]))
-
-    fine_w = second(c, s, LANES // STRIDE)
-    coarse_w = second(np.repeat(c, 2, axis=0), np.repeat(s, 2, axis=0), LANES // (2 * STRIDE))
+
+    def weights(y, is_imag):
+        c, s = trig(y[:, None] * freq)
+        from_real = np.concatenate([c, -s, -s, -c], axis=1)
+        from_imag = np.concatenate([s, c, c, -s], axis=1)
+        return rounded(np.where(is_imag[:, None], from_imag, from_real))
+
+    fine_w = np.concatenate([np.concatenate([weights(*w)] * 2, axis=0) for w in windows], axis=0)
+    both = np.arange(2 * LANES) >= LANES
+    coarse_w = np.concatenate(
+        [weights(np.concatenate([at // 2] * 2), both) for at in (lane, (lane + half) % LANES)], axis=0
+    )
 
     shift = np.arange(WINDOW) - WINDOW // 2
-    c, s = trig(np.arange(PATCH)[:, None] * shift[None, :])
-    c, s = block_diagonal(c, 4), block_diagonal(s, 4)
-    inverse = rounded(np.block([[c, s], [-s, c]]))
-
-    weight = np.where((k == 0) | (k == PATCH // 2), 1.0, 2.0) * keep
-    c, s = trig(shift[:, None] * np.arange(KP)[None, :])
+    c, s = trig((np.arange(LANES) % PATCH)[:, None] * shift[None, :])
+    inverse = []
+    for p in range(4):
+        block = np.zeros((2 * LANES, 2 * LANES))
+        block[:LANES, WINDOW * p : WINDOW * (p + 1)] = c
+        block[:LANES, LANES + WINDOW * p : LANES + WINDOW * (p + 1)] = s
+        block[LANES:, WINDOW * p : WINDOW * (p + 1)] = -s
+        block[LANES:, LANES + WINDOW * p : LANES + WINDOW * (p + 1)] = c
+        inverse.append(rounded(block))
+
+    weight = np.where(k == PATCH // 2, 1.0, 2.0)
+    c, s = trig(shift[:, None] * k.T)
     last_high, last_low = split(np.concatenate([c * weight.T, -s * weight.T], axis=1))
     last = np.concatenate([last_high, last_high, last_low], axis=1)
-    energy = np.kron(np.eye(4), np.ones((PATCH, WINDOW)))
-    return [
-        fine_w,
-        coarse_w,
-        inverse,
-        last,
-        np.asarray(energy, np.float32).astype(BF16),
-        np.asarray(np.broadcast_to(weight, (KP, LANES)), np.float32),
-        *firsts,
-    ]
+    return [fine_w, coarse_w, np.concatenate(inverse, axis=0), last, *firsts]
 
 
 def split_value(value):
@@ -119,73 +128,114 @@
     return jnp.dot(a, b, preferred_element_type=F32)
 
 
-def section_spectra(pixels, first, fine_w, coarse_w, fine_rows, coarse_rows):
-    half = matmul(first, jnp.concatenate([pixels, pixels], axis=0))
-    width = half.shape[1]
-    tiles = width // LANES
-    row = lax.broadcasted_iota(jnp.int32, (KP, width), 0)
-    fine_in, coarse_in = [], []
-    for unit in range(fine_rows + coarse_rows):
-        real = half[2 * KP * unit : 2 * KP * unit + KP]
-        imag = half[2 * KP * unit + KP : 2 * KP * (unit + 1)]
-        sums = real[0:1]
-        high = sums.astype(BF16).astype(F32)
-        middle = (sums - high).astype(BF16).astype(F32)
-        low = sums - high - middle
-        real = jnp.where(row == 0, high, real)
-        real = jnp.where(row == HALF, middle, real)
-        real = jnp.where(row == HALF + 1, low, real)
-        target = fine_in if unit < fine_rows else coarse_in
-        for tile in range(tiles):
-            at = slice(LANES * tile, LANES * (tile + 1))
-            target.append(jnp.concatenate([real[:, at], imag[:, at]], axis=1))
-
-    def transform(parts, weights):
-        high, low = split_value(jnp.concatenate(parts, axis=0))
-        return matmul(high, weights) + matmul(low, weights)
-
-    fine = transform(fine_in, fine_w) if fine_rows else None
-    coarse = transform(coarse_in, coarse_w) if coarse_rows else None
-    wide = 2 * LANES
-    lane = lax.broadcasted_iota(jnp.int32, (KP, wide), 1)
-    krow = lax.broadcasted_iota(jnp.int32, (KP, wide), 0)
-    sign = jnp.where(lane % 2 == 0, 1.0, -1.0).astype(F32)
-    dc = (krow == 0) & (lane % PATCH == 0)
-
-    def finish(parts, rows):
-        count = len(parts) // rows
-        rolled = [pltpu.roll(part, wide - PATCH, 1) for part in parts]
-        done = []
-        for index, part in enumerate(parts):
-            if index % count == count - 1:
-                following = jnp.where(lane < wide - PATCH, rolled[index], 0.0)
-            else:
-                following = jnp.where(lane < wide - PATCH, rolled[index], rolled[index + 1])
-            value = part + sign * following
-            value = jnp.where(krow == 0, value + value[HALF : HALF + 1] + value[HALF + 1 : HALF + 2], value)
-            value = jnp.where(dc, 0.0, value)
-            done.append(value)
-        return done
-
-    def groups(offset):
-        fine_parts = [
-            fine[KP * g : KP * (g + 1), offset * wide : (offset + 1) * wide]
-            for g in range(fine_rows * tiles)
-        ]
-        coarse_parts = [
-            jnp.concatenate(
-                [
-                    coarse[KP * g : KP * (g + 1), offset * LANES : (offset + 1) * LANES],
-                    coarse[KP * (g + 1) : KP * (g + 2), offset * LANES : (offset + 1) * LANES],
-                ],
-                axis=1,
-            )
-            for g in range(0, coarse_rows * tiles, 2)
-        ]
-        done = finish(fine_parts, fine_rows) if fine_rows else []
-        return done + (finish(coarse_parts, coarse_rows) if coarse_rows else [])
-
-    return groups(0), groups(1)
+def lanes_of(shape):
+    return lax.broadcasted_iota(jnp.int32, shape, 1)
+
+
+def rows_of(shape):
+    return lax.broadcasted_iota(jnp.int32, shape, 0)
+
+
+def tiles_of(value):
+    return [value[:, LANES * t : LANES * (t + 1)] for t in range(value.shape[1] // LANES)]
+
+
+def window(kind, real, turned, real_next, turned_next):
+    lane = lanes_of(real.shape)
+    half, quarter = LANES // 2, LANES // 4
+    if kind == 0:
+        return jnp.where(lane < half, real, turned)
+    if kind == 1:
+        return jnp.where((lane >= quarter) & (lane < 3 * quarter), real, turned)
+    if kind == 2:
+        return jnp.where(lane < half, turned, real)
+    left = jnp.where(lane < quarter, real_next, turned)
+    right = jnp.where(lane < 3 * quarter, turned_next, real)
+    return jnp.where(lane < half, left, right)
+
+
+def sum_rows(value):
+    row = rows_of((8, LANES))
+    tiles = tiles_of(value)
+    tiles.append(jnp.zeros_like(tiles[0]))
+    count = len(tiles) - 1
+
+    def spread(parts):
+        out = parts[count - 1]
+        for t in range(count - 1):
+            out = jnp.where(row % count == t, parts[t], out)
+        return out
+
+    return spread(tiles[:-1]), spread(tiles[1:])
+
+
+def sum_parts(value, count):
+    first = rows_of(value.shape) < count
+    high, rest = split_value(value)
+    high = high.astype(F32)
+    middle = rest.astype(F32)
+    low = value - high - middle
+    return jnp.where(first, high, low).astype(BF16), jnp.where(first, middle, 0.0).astype(BF16)
+
+
+def section_spectra(pixels, first, fine_w_ref, coarse_w_ref, fine_rows, coarse_rows, columns):
+    rows = matmul(first, jnp.concatenate([pixels, pixels], axis=0))
+    units = fine_rows + coarse_rows
+    count = rows.shape[1] // LANES
+    zero = jnp.zeros((SLOTS, LANES), BF16)
+    blank = jnp.zeros((8, LANES), F32)
+    done = []
+
+    def finish(out):
+        sums = out[SLOTS * count : SLOTS * count + 8]
+        sums = sums + pltpu.roll(sums, 4, 0)
+        sums = jnp.where(lanes_of(sums.shape) % PATCH == 0, 0.0, sums)
+        done.append((out, sums))
+
+    for unit in range(units):
+        real = tiles_of(rows[2 * SLOTS * unit : 2 * SLOTS * unit + SLOTS])
+        imag = tiles_of(rows[2 * SLOTS * unit + SLOTS : 2 * SLOTS * (unit + 1)])
+        if unit < fine_rows:
+            imag = [pltpu.roll(tile, LANES // 2, 1) for tile in imag]
+        real = [split_value(tile) for tile in real] + [(zero, zero)]
+        imag = [split_value(tile) for tile in imag] + [(zero, zero)]
+        at = 2 * SLOTS * units + 8 * unit
+        now, following = sum_rows(rows[at : at + 8])
+        if unit < fine_rows:
+            for kind in range(4):
+                lhs = [
+                    jnp.concatenate(
+                        [window(kind, real[t][h], imag[t][h], real[t + 1][h], imag[t + 1][h]) for h in range(2)], axis=1
+                    )
+                    for t in range(count)
+                ]
+                sums = sum_parts(window(kind, now, blank, following, blank), count)
+                lhs.append(jnp.concatenate(sums, axis=1))
+                weights = fine_w_ref[2 * LANES * kind : 2 * LANES * (kind + 1), :columns]
+                finish(matmul(jnp.concatenate(lhs, axis=0), weights))
+        else:
+            lower = lanes_of((SLOTS, LANES)) < LANES // 2
+            low_sums = lanes_of((8, LANES)) < LANES // 2
+            for kind in range(2):
+                sums = sum_parts(jnp.where(low_sums, following, now) if kind else now, count)
+                weights = coarse_w_ref[2 * LANES * kind : 2 * LANES * (kind + 1), :columns]
+                out = None
+                for h in range(2):
+                    lhs = [
+                        jnp.concatenate(
+                            [
+                                jnp.where(lower, part[t + 1][h], part[t][h]) if kind else part[t][h]
+                                for part in (real, imag)
+                            ],
+                            axis=1,
+                        )
+                        for t in range(count)
+                    ]
+                    lhs.append(jnp.concatenate([sums[h], jnp.zeros_like(sums[h])], axis=1))
+                    term = matmul(jnp.concatenate(lhs, axis=0), weights)
+                    out = term if out is None else out + term
+                finish(out)
+    return done
 
 
 def block_transpose(value):
@@ -205,9 +255,9 @@
     pixels_ref, fine_mask_ref, coarse_mask_ref = refs[:3]
     sources = refs[3 : 3 + const_count]
     fine_out_ref, coarse_out_ref = refs[3 + const_count : 5 + const_count]
-    main_ref, rim_ref, real_ref, imag_ref, scale_ref = refs[5 + const_count : 10 + const_count]
-    held = refs[10 + const_count : 10 + 2 * const_count]
-    own_sem, const_sem, send_sem, main_sem, rim_sem = refs[10 + 2 * const_count :]
+    main_ref, rim_ref, own_ref, scale_ref = refs[5 + const_count : 9 + const_count]
+    held = refs[9 + const_count : 9 + 2 * const_count]
+    own_sem, const_sem, send_sem, main_sem, rim_sem = refs[9 + 2 * const_count :]
     sec, strip = lax.axis_index("sec"), lax.axis_index("strip")
     secs, strips = lax.axis_size("sec"), lax.axis_size("strip")
     even, odd = strip % 2 == 0, strip % 2 == 1
@@ -290,11 +340,14 @@
     coarse_rows, coarse_cols = coarse_mask_ref.shape[1:]
     fine_groups = fine_rows * fine_cols // 4
     count = fine_groups + coarse_rows * coarse_cols // 4
-    fine_w_ref, coarse_w_ref, inverse_ref, last_ref, energy_ref, weight_ref = held[:6]
-    first_refs = held[6:]
+    fine_w_ref, coarse_w_ref, inverse_ref, last_ref = held[:4]
+    first_refs = held[4:]
     inner = inner_rows(pixels_ref.shape[1])
-    inner_groups = inner * fine_cols // 4
-    bounds = {"inner": (0, inner_groups), "outer": (inner_groups, count)}
+    tiles = pixels_ref.shape[2] // LANES
+    bounds = {
+        "inner": (0, inner * tiles, 0),
+        "outer": (inner * tiles, count, 4 * inner),
+    }
     gain = table_gain()
 
     def spread(mask, cols):
@@ -312,54 +365,110 @@
         for t in range(m.shape[1] // LANES)
     ]
 
+    def squares(out, sums):
+        row = rows_of((8, LANES))
+        extra = sums * sums * 0.5
+        parts = []
+        for t in range(tiles):
+            block = out[SLOTS * t : SLOTS * (t + 1)]
+            block = block * block
+            total = jnp.where(row == 0, 0.5 * block[:8], block[:8])
+            for r in range(8, SLOTS, 8):
+                total = total + block[r : r + 8]
+            total = total + jnp.where(row == t, extra, 0.0)
+            parts.append(jnp.sum(total, axis=1, keepdims=True))
+        return parts
+
+    def members(blocks, coarse):
+        if not coarse:
+            return [[(kind, t) for kind in range(4)] for t in range(tiles)]
+        return [[(p % 2, 2 * g + p // 2) for p in range(4)] for g in range(tiles // 2)]
+
+    def units_of(spectra, part):
+        number = (inner if part == "inner" else fine_rows - inner) * 4
+        found = [(spectra[at : at + 4], False) for at in range(0, number, 4)]
+        return found + [(spectra[at : at + 2], True) for at in range(number, len(spectra), 2)]
+
     def analyse(section, part):
-        start, stop = bounds[part]
+        start, stop, block = bounds[part]
         if start == stop:
             return
-        weight = jnp.concatenate([weight_ref[...]] * 2, axis=1)
         if part == "inner":
             pixels, rows = main_ref[section], (inner, 0)
         else:
             pixels = jnp.concatenate([main_ref[section], rim_ref[section]], axis=0)
             rows = (fine_rows - inner, coarse_rows)
         first = first_refs[0 if part == "inner" else -1][...]
-        real, imag = section_spectra(pixels, first, fine_w_ref[...], coarse_w_ref[...], *rows)
-        sums = []
-        for g in range(start, stop):
-            re, im = real[g - start], imag[g - start]
-            real_ref[section, KP * g : KP * (g + 1)] = re
-            imag_ref[section, KP * g : KP * (g + 1)] = im
-            sums.append(jnp.sum(weight * (re * re + im * im), axis=0, keepdims=True))
-        sums = jnp.concatenate(sums, axis=0)
-        high, rest = split_value(sums)
-        low = (sums - high.astype(F32) - rest.astype(F32)).astype(BF16)
-        energy = energy_ref[...]
-        total = matmul(high, energy) + matmul(rest, energy) + matmul(low, energy)
-        scale = 1.0 / jnp.sqrt(total * (1.0 / (float(PATCH) ** 4 * gain * gain)) + 1e-05)
-        scale_ref[section, start:stop] = scale
-
-    def correlate(d, part):
-        start, stop = bounds[part]
-        if start == stop:
+        columns = LANES if section == 0 else 2 * LANES
+        spectra = section_spectra(pixels, first, fine_w_ref, coarse_w_ref, *rows, columns)
+        lane = lanes_of((8, LANES)) // WINDOW
+        totals = []
+        for blocks, coarse in units_of(spectra, part):
+            powers = [squares(out[:, :LANES], sums[:, :LANES]) for out, sums in blocks]
+            for group in members(blocks, coarse):
+                kind, t = group[3]
+                total = jnp.broadcast_to(powers[kind][t], (8, LANES))
+                for p in range(3):
+                    kind, t = group[p]
+                    total = jnp.where(lane == p, powers[kind][t], total)
+                totals.append(jnp.sum(total, axis=0, keepdims=True))
+        total = jnp.concatenate(totals, axis=0)
+        scale = 1.0 / jnp.sqrt(total * (2.0 / (float(PATCH) ** 4 * gain * gain)) + 1e-05)
+        if section == 0:
+            scale_ref[start:stop] = scale
+            for index, (out, sums) in enumerate(spectra):
+                own_ref[block + index, : SLOTS * tiles] = out[: SLOTS * tiles]
+                own_ref[block + index, SLOTS * tiles :] = sums
             return
-        rows = slice(KP * start, KP * stop)
-        own_real, own_imag = real_ref[0, rows], imag_ref[0, rows]
-        other_real, other_imag = real_ref[d, rows], imag_ref[d, rows]
-        cross_real = own_real * other_real + own_imag * other_imag
-        cross_imag = own_real * other_imag - own_imag * other_real
-        cross = jnp.concatenate([cross_real.astype(BF16), cross_imag.astype(BF16)], axis=1)
-        rows = matmul(cross, inverse_ref[...])
+        correlate(section, part, spectra, scale)
+
+    def correlate(d, part, spectra, other_scale):
+        start, stop, block = bounds[part]
+        row = rows_of((8, LANES))
+        lhs, group_rows, sum_at = [], [], []
+        at = 0
+        for blocks, coarse in units_of(spectra, part):
+            products = []
+            for index, (out, sums) in enumerate(blocks):
+                own = own_ref[block + index]
+                own_rows, own_sums = own[: SLOTS * tiles], own[SLOTS * tiles :]
+                body = [(own_rows * tile).astype(BF16) for tile in tiles_of(out[: SLOTS * tiles])]
+                tail = [own_sums * tile for tile in tiles_of(sums)]
+                products.append((body, tail))
+            block += len(blocks)
+            groups = members(blocks, coarse)
+            pieces = []
+            for p in range(4):
+                body = [
+                    jnp.concatenate([x[SLOTS * t : SLOTS * (t + 1)] for x in products[kind][0]], axis=1)
+                    for kind, t in (group[p] for group in groups)
+                ]
+                tail = products[groups[0][p][0]][1]
+                if coarse:
+                    tail = [jnp.where(row % 2 == p // 2, x, 0.0) for x in tail]
+                body.append(jnp.concatenate([x.astype(BF16) for x in tail], axis=1))
+                pieces.append(jnp.concatenate(body, axis=0))
+            lhs.append(jnp.concatenate(pieces, axis=1))
+            for g in range(len(groups)):
+                group_rows.append(at + SLOTS * g)
+                base = at + SLOTS * len(groups)
+                sum_at.append([base + 2 * g, base + 2 * g + 1] if coarse else [base + g])
+            at += SLOTS * len(groups) + 8
+        rows = jnp.concatenate([matmul(x, inverse_ref[...]) for x in lhs], axis=0)
         stacked = []
-        for g in range(stop - start):
-            piece = rows[KP * g : KP * (g + 1)]
+        for r in group_rows:
+            piece = rows[r : r + SLOTS]
             stacked.append(jnp.concatenate([piece[:, :LANES], piece[:, LANES:]], axis=0))
         high, low = split_value(jnp.concatenate(stacked, axis=1))
         maps = matmul(last_ref[...], jnp.concatenate([high, low, high], axis=0))
-        both = scale_ref[0, start:stop] * scale_ref[d, start:stop] * (1.0 / (float(PATCH) ** 3 * gain**3))
+        both = scale_ref[start:stop] * other_scale * (1.0 / (float(PATCH) ** 3 * gain**3))
         for g in range(start, stop):
             at = g - start
             scale = both[at : at + 1] * masks[g]
-            value = block_transpose(maps[:, LANES * at : LANES * (at + 1)] * scale)
+            value = maps[:, LANES * at : LANES * (at + 1)]
+            for r in sum_at[at]:
+                value = value + rows[r : r + 1, :LANES]
+            value = block_transpose(value * scale)
             if g < fine_groups:
                 ref, local_g, cols = fine_out_ref, g, fine_cols
             else:
@@ -403,18 +512,11 @@
             far_relay[c].wait_recv()
             pl.when(odd)(far_rim_across[c].start)
 
-    @pl.when(has_near)
-    def _():
-        correlate(1, "inner")
-        correlate(1, "outer")
-
     @pl.when(has_far)
     def _():
         analyse(2, "inner")
-        correlate(2, "inner")
         each(below, far_rim_relay, "wait_recv")
         analyse(2, "outer")
-        correlate(2, "outer")
 
     pl.when(jnp.logical_not(has_near))(lambda: clear(1))
     pl.when(jnp.logical_not(has_far))(lambda: clear(2))
@@ -446,6 +548,7 @@
     fine_rows, fine_cols = mask_fine.shape[1:]
     coarse_rows, coarse_cols = mask_coarse.shape[1:]
     count = (fine_rows * fine_cols + coarse_rows * coarse_cols) // 4
+    blocks = 4 * fine_rows + 2 * coarse_rows
     vmem = pl.BlockSpec(memory_space=pltpu.VMEM)
     anywhere = pl.BlockSpec(memory_space=pl.ANY)
     flat = WINDOW * WINDOW
@@ -462,9 +565,8 @@
         scratch_shapes=[
             pltpu.VMEM((3, strip_rows, width), BF16),
             pltpu.VMEM((3, strip_rows, width), BF16),
-            pltpu.VMEM((3, KP * count, 2 * LANES), F32),
-            pltpu.VMEM((3, KP * count, 2 * LANES), F32),
-            pltpu.VMEM((3, count, LANES), F32),
+            pltpu.VMEM((blocks, SLOTS * (width // LANES) + 8, LANES), F32),
+            pltpu.VMEM((count, LANES), F32),
             *[pltpu.VMEM(c.shape, c.dtype) for c in consts],
             pltpu.SemaphoreType.DMA,
             pltpu.SemaphoreType.DMA((len(consts),)),

time: 13.7 us -> 13 us (0.949)
  Pallas kernels: 12.9 us -> 12.2 us
    pallas_call x1, Pallas kernels: 12.2 us -> 11.5 us  [local(): pl.pallas_call(functools.partial(compute, len(consts)), out_shape=shapes,...]
where the time goes in v3:
time: 13 us; the launch traced here: 12.9 us
  Pallas kernels  12.2 us (94%)
  between operations  0.64 us (5%)
    pallas_call x1, Pallas kernels, local(): pl.pallas_call(functools.partial(compute, len(consts)), out_shape=shapes,...  11.5 us
    pallas_call x1, Pallas kernels, local(): pl.pallas_call(deliver, out_shape=shapes, in_specs=[vmem, vmem], out_spec...  0.75 us

profile of v3, /device:TPU:0, one launch (start us, length us, event | category | flops | bytes accessed | tf_op | source)
XLA Modules:
  0.0 12.9 jit_solution(273911816770961908)
XLA Ops:
  0.6 11.5 %shard_map.104 = (f32[1,2,2,16,1024]{4,3,2,1,0:T(8,128)S(1)}, f32[1,2,1,8,1024]{4,3,2,1,0:T(8,128)S(1)}) custom-call(bf16[1,64,512]{2,1,0:T(8,128)(2,1)} %refs_0_.1, s32[1,2,16]{2,1,0:T(2,128)} %refs_1_.1, s32[1,1,8]{2,1,0:T(1,128)} %refs_2_.1, bf16[1024,256]{1,0:T(8,128)(2,1)} %constant.12.clone.refs_3_, bf16[512,256]{1,0:T(8,128)(2,1)} %constant.13.clone.refs_4_, ...), custom_call_target="tpu_custom_call" | custom-call | tf_op jit(solution)/shard_map/pallas_call | solution.py:560
  12.1 0.7 %shard_map.105 = (f32[1,2,2,16,1024]{4,3,2,1,0:T(8,128)}, f32[1,2,1,8,1024]{4,3,2,1,0:T(8,128)}) custom-call(f32[1,2,2,16,1024]{4,3,2,1,0:T(8,128)S(1)} %get-tuple-element.4.fine_ref, f32[1,2,1,8,1024]{4,3,2,1,0:T(8,128)S(1)} %get-tuple-element.5.coarse_ref), custom_call_target="tpu_custom_call" | custom-call | tf_op jit(solution)/shard_map/pallas_call | solution.py:579

commit v4 on v3

--- a/solution.py
+++ b/solution.py
@@ -251,13 +251,17 @@
     return jnp.where((row % 2) == (block % 2), value, other)
 
 
+def consts_order(const_count):
+    return (4, 0, *range(5, const_count), 1, 2, 3)
+
+
 def compute(const_count, *refs):
-    pixels_ref, fine_mask_ref, coarse_mask_ref = refs[:3]
+    pixels_ref, fine_source_ref, coarse_source_ref = refs[:3]
     sources = refs[3 : 3 + const_count]
     fine_out_ref, coarse_out_ref = refs[3 + const_count : 5 + const_count]
-    main_ref, rim_ref, own_ref, scale_ref = refs[5 + const_count : 9 + const_count]
-    held = refs[9 + const_count : 9 + 2 * const_count]
-    own_sem, const_sem, send_sem, main_sem, rim_sem = refs[9 + 2 * const_count :]
+    main_ref, rim_ref, own_ref, scale_ref, fine_mask_ref, coarse_mask_ref = refs[5 + const_count : 11 + const_count]
+    held = refs[11 + const_count : 11 + 2 * const_count]
+    own_sem, mask_sem, const_sem, send_sem, main_sem, rim_sem = refs[11 + 2 * const_count :]
     sec, strip = lax.axis_index("sec"), lax.axis_index("strip")
     secs, strips = lax.axis_size("sec"), lax.axis_size("strip")
     even, odd = strip % 2 == 0, strip % 2 == 1
@@ -282,7 +286,15 @@
         pltpu.make_async_copy(source, target, const_sem.at[index])
         for index, (source, target) in enumerate(zip(sources, held))
     ]
-    for copy in const_copies:
+    for index in consts_order(const_count):
+        const_copies[index].start()
+    mask_copies = [
+        pltpu.make_async_copy(source, target, mask_sem.at[index])
+        for index, (source, target) in enumerate(
+            ((fine_source_ref, fine_mask_ref), (coarse_source_ref, coarse_mask_ref))
+        )
+    ]
+    for copy in mask_copies:
         copy.start()
 
     diagonal = even & (sec >= 1) & (strip >= 1)
@@ -356,14 +368,15 @@
         picks = jnp.where(source == target, 1.0, 0.0).astype(BF16)
         return matmul(mask.astype(F32).astype(BF16), picks)
 
-    fine_mask = spread(fine_mask_ref[0], fine_cols)
-    coarse_mask = spread(coarse_mask_ref[0], coarse_cols)
-    masks = [
-        m[r : r + 1, LANES * t : LANES * (t + 1)]
-        for m in (fine_mask, coarse_mask)
-        for r in range(m.shape[0])
-        for t in range(m.shape[1] // LANES)
-    ]
+    def mask_rows():
+        fine_mask = spread(fine_mask_ref[0], fine_cols)
+        coarse_mask = spread(coarse_mask_ref[0], coarse_cols)
+        return [
+            m[r : r + 1, LANES * t : LANES * (t + 1)]
+            for m in (fine_mask, coarse_mask)
+            for r in range(m.shape[0])
+            for t in range(m.shape[1] // LANES)
+        ]
 
     def squares(out, sums):
         row = rows_of((8, LANES))
@@ -482,9 +495,14 @@
             ref[0, d - 1] = jnp.zeros(ref.shape[2:], F32)
 
     own_copy.wait()
-    for copy in const_copies:
+    for index in consts_order(const_count)[:2]:
+        const_copies[index].wait()
+    analyse(0, "inner")
+    for index in consts_order(const_count)[2:]:
+        const_copies[index].wait()
+    for copy in mask_copies:
         copy.wait()
-    analyse(0, "inner")
+    masks = mask_rows()
     @pl.when(has_near)
     def _():
         for c in range(CHUNKS):
@@ -560,15 +578,18 @@
     maps = pl.pallas_call(
         functools.partial(compute, len(consts)),
         out_shape=shapes,
-        in_specs=[anywhere, vmem, vmem] + [anywhere] * len(consts),
+        in_specs=[anywhere] * (3 + len(consts)),
         out_specs=(vmem, vmem),
         scratch_shapes=[
             pltpu.VMEM((3, strip_rows, width), BF16),
             pltpu.VMEM((3, strip_rows, width), BF16),
             pltpu.VMEM((blocks, SLOTS * (width // LANES) + 8, LANES), F32),
             pltpu.VMEM((count, LANES), F32),
+            pltpu.VMEM(mask_fine.shape, mask_fine.dtype),
+            pltpu.VMEM(mask_coarse.shape, mask_coarse.dtype),
             *[pltpu.VMEM(c.shape, c.dtype) for c in consts],
             pltpu.SemaphoreType.DMA,
+            pltpu.SemaphoreType.DMA((2,)),
             pltpu.SemaphoreType.DMA((len(consts),)),
             pltpu.SemaphoreType.DMA((8, CHUNKS)),
             pltpu.SemaphoreType.DMA((3, CHUNKS)),

time: 13 us -> 12.4 us (0.954)
  Pallas kernels: 12.2 us -> 11.6 us
    pallas_call x1, Pallas kernels: 11.5 us -> 10.9 us  [local(): pl.pallas_call(functools.partial(compute, len(consts)), out_shape=shapes,...]
where the time goes in v4:
time: 12.4 us; the launch traced here: 12.3 us
  Pallas kernels  11.6 us (94%)
  between operations  0.64 us (5%)
    pallas_call x1, Pallas kernels, local(): pl.pallas_call(functools.partial(compute, len(consts)), out_shape=shapes,...  10.9 us
    pallas_call x1, Pallas kernels, local(): pl.pallas_call(deliver, out_shape=shapes, in_specs=[vmem, vmem], out_spec...  0.75 us

profile of v4, /device:TPU:0, one launch (start us, length us, event | category | flops | bytes accessed | tf_op | source)
XLA Modules:
  0.0 12.3 jit_solution(743184603318415791)
XLA Ops:
  0.6 10.9 %shard_map.104 = (f32[1,2,2,16,1024]{4,3,2,1,0:T(8,128)S(1)}, f32[1,2,1,8,1024]{4,3,2,1,0:T(8,128)S(1)}) custom-call(bf16[1,64,512]{2,1,0:T(8,128)(2,1)} %refs_0_.1, s32[1,2,16]{2,1,0:T(2,128)} %refs_1_.1, s32[1,1,8]{2,1,0:T(1,128)} %refs_2_.1, bf16[1024,256]{1,0:T(8,128)(2,1)} %constant.12.clone.refs_3_, bf16[512,256]{1,0:T(8,128)(2,1)} %constant.13.clone.refs_4_, ...), custom_call_target="tpu_custom_call" | custom-call | tf_op jit(solution)/shard_map/pallas_call | solution.py:578
  11.5 0.7 %shard_map.105 = (f32[1,2,2,16,1024]{4,3,2,1,0:T(8,128)}, f32[1,2,1,8,1024]{4,3,2,1,0:T(8,128)}) custom-call(f32[1,2,2,16,1024]{4,3,2,1,0:T(8,128)S(1)} %get-tuple-element.4.fine_ref, f32[1,2,1,8,1024]{4,3,2,1,0:T(8,128)S(1)} %get-tuple-element.5.coarse_ref), custom_call_target="tpu_custom_call" | custom-call | tf_op jit(solution)/shard_map/pallas_call | solution.py:600

commit v5 on v4

--- a/solution.py
+++ b/solution.py
@@ -275,9 +275,9 @@
         def _():
             pl.semaphore_signal(barrier, inc=1, device_id=device, device_id_type=MESH)
 
+    greet(has_near, {"sec": sec + 1})
     greet(even & has_far, {"sec": sec + 2})
     greet(odd & has_near & below, {"sec": sec + 1, "strip": strip + 1})
-    greet(has_near, {"sec": sec + 1})
     greet(below, {"strip": strip + 1})
 
     own_copy = pltpu.make_async_copy(pixels_ref.at[0], main_ref.at[0], own_sem)
@@ -339,9 +339,10 @@
             for copy in copies:
                 getattr(copy, method)()
 
+    each(odd & (sec >= 1), near_send, "start")
     each(strip >= 1, rim_send, "start")
     each(diagonal, diagonal_send, "start")
-    each(sec >= 1, near_send, "start")
+    each(even & (sec >= 1), near_send, "start")
     each(routed, routed_send, "start")
 
     @pl.when(jnp.logical_not(below))
@@ -510,17 +511,20 @@
             pl.when(odd & (sec >= 1))(far_relay[c].start)
             pl.when(odd)(near_rim_relay[c].start)
 
+    passes = odd & (sec >= 1)
+
+    @pl.when(has_near & below & passes)
+    def _():
+        for c in range(CHUNKS):
+            near_rim_relay[c].wait_recv()
+            far_rim_relay[c].start()
+
     each(below, rim_send, "wait_recv")
     analyse(0, "outer")
 
     @pl.when(has_near)
     def _():
-        @pl.when(below)
-        def _():
-            for c in range(CHUNKS):
-                near_rim_relay[c].wait_recv()
-                pl.when(odd & (sec >= 1))(far_rim_relay[c].start)
-
+        each(below & jnp.logical_not(passes), near_rim_relay, "wait_recv")
         analyse(1, "inner")
         analyse(1, "outer")
 

time: 12.4 us -> 12.4 us (level)
  no operation moved by 1% of the time
where the time goes in v5:
time: 12.4 us; the launch traced here: 12.3 us
  Pallas kernels  11.6 us (94%)
  between operations  0.64 us (5%)
    pallas_call x1, Pallas kernels, local(): pl.pallas_call(functools.partial(compute, len(consts)), out_shape=shapes,...  10.9 us
    pallas_call x1, Pallas kernels, local(): pl.pallas_call(deliver, out_shape=shapes, in_specs=[vmem, vmem], out_spec...  0.75 us

profile of v5, /device:TPU:0, one launch (start us, length us, event | category | flops | bytes accessed | tf_op | source)
XLA Modules:
  0.0 12.3 jit_solution(7085896514552539026)
XLA Ops:
  0.6 10.9 %shard_map.104 = (f32[1,2,2,16,1024]{4,3,2,1,0:T(8,128)S(1)}, f32[1,2,1,8,1024]{4,3,2,1,0:T(8,128)S(1)}) custom-call(bf16[1,64,512]{2,1,0:T(8,128)(2,1)} %refs_0_.1, s32[1,2,16]{2,1,0:T(2,128)} %refs_1_.1, s32[1,1,8]{2,1,0:T(1,128)} %refs_2_.1, bf16[1024,256]{1,0:T(8,128)(2,1)} %constant.12.clone.refs_3_, bf16[512,256]{1,0:T(8,128)(2,1)} %constant.13.clone.refs_4_, ...), custom_call_target="tpu_custom_call" | custom-call | tf_op jit(solution)/shard_map/pallas_call | solution.py:582
  11.5 0.7 %shard_map.105 = (f32[1,2,2,16,1024]{4,3,2,1,0:T(8,128)}, f32[1,2,1,8,1024]{4,3,2,1,0:T(8,128)}) custom-call(f32[1,2,2,16,1024]{4,3,2,1,0:T(8,128)S(1)} %get-tuple-element.4.fine_ref, f32[1,2,1,8,1024]{4,3,2,1,0:T(8,128)S(1)} %get-tuple-element.5.coarse_ref), custom_call_target="tpu_custom_call" | custom-call | tf_op jit(solution)/shard_map/pallas_call | solution.py:604
